TPU v7x, 32 devices: a whole 2x2x4 slice. The times are simulated.
32 devices in a mesh: phase: 4 (over x, core), seq: 4 (over z), mp: 2 (over y).
Axes of the slice: x: 2, y: 2, z: 4, core: 2. Of those that a mesh axis runs over, the one named last changes fastest.
Arguments:
- queries: bfloat16 [4, 2048, 4096], P('phase', 'seq', 'mp'), may hold values from -360 to 360
- key_weight: bfloat16 [4, 1024, 4096], P('phase', None, 'mp'), may hold values from -0.1875 to 0.1875
- value_weight: bfloat16 [4, 1024, 4096], P('phase', None, 'mp'), may hold values from -0.1875 to 0.1875
- enc_gain: float32 [1024], replicated, may hold values from 0.25 to 2
- neighbour_states: bfloat16 [80, 64, 1024], P('seq', ('phase', 'mp')), may hold values from -600 to 600
- slot_dest: int32 [80], P('seq'), may hold values from -1 to 63, as said below
Outputs:
- context: bfloat16 [4, 2048, 4096], P('phase', 'seq', 'mp')
Inputs may be any that keep to these rules, and one draw needn't show every extreme that they name: slot_dest names every position 0 to 63 exactly once and is -1 elsewhere. Positions 2 * 8 j to 2 * 8 (j + 1) - 1 belong to the tokens of index j of seq. The slots of one index of seq name at most 5 positions of any one index of seq, and this bound is reached; one index of seq has up to 20 filled slots, reached in every draw.
All inputs are finite; a program needn't handle non-finite values.
Results may differ from a plain program's by a relative error of at most 0.0074.
Values may be sent and summed in bfloat16 or wider, within the bound.
No kernel may reach another device: no remote copies, remote signals or barrier semaphores. Data moves between devices by JAX's collectives and lax.ppermute only.
A program may use at most 64 MiB of HBM per device.

v0:
```python
import jax
import jax.numpy as jnp
from jax import lax
from jax.sharding import PartitionSpec as P

HD = 128
SEGLEN = 64
NLEN = 64
NEIGH = 2


def shifted(shard, axis, by):
    peers = lax.axis_size(axis)
    pairs = [(i, i + by) for i in range(peers) if 0 <= i + by < peers]
    return lax.ppermute(shard, axis, pairs)


def normalize(rows, gain):
    states = rows.astype(jnp.float32)
    meansq = jnp.mean(states * states, axis=-1, keepdims=True)
    return (states * lax.rsqrt(meansq + 1e-06) * gain).astype(jnp.bfloat16)


def project(rows, weight):
    flattened = rows.reshape(-1, rows.shape[-1])
    return jnp.dot(flattened, weight, preferred_element_type=jnp.float32).astype(jnp.bfloat16)


def attend(query_win, key_win, value_win):
    windows = query_win.shape[0]
    heads = query_win.shape[2] // HD
    query_four = query_win.reshape(windows, query_win.shape[1], heads, HD)
    key_four = key_win.reshape(windows, key_win.shape[1], heads, HD)
    value_four = value_win.reshape(windows, value_win.shape[1], heads, HD)
    scores = jnp.einsum(
        "wqhd,wkhd->whqk", query_four, key_four, preferred_element_type=jnp.float32
    ) * HD ** (-0.5)
    top = jnp.max(scores, axis=-1, keepdims=True)
    exponent = jnp.exp(scores - top)
    weights = (exponent / jnp.sum(exponent, axis=-1, keepdims=True)).astype(jnp.bfloat16)
    context = jnp.einsum("whqk,wkhd->wqhd", weights, value_four, preferred_element_type=jnp.float32)
    return context.astype(jnp.bfloat16).reshape(windows, query_win.shape[1], heads * HD)


def packing(slot_dest, shards, per_shard, capacity):
    count = slot_dest.shape[0]
    is_live = slot_dest >= 0
    target = jnp.where(is_live, slot_dest // per_shard, -1)
    order = jnp.arange(count)
    earlier = (target[:, None] == target[None, :]) & (order[None, :] < order[:, None])
    slot_rank = jnp.sum(earlier.astype(jnp.int32), axis=1)
    buffer_slot = jnp.where(is_live, target * capacity + slot_rank, -1)
    matches = jnp.arange(shards * capacity)[:, None] == buffer_slot[None, :]
    selector = matches.astype(jnp.bfloat16)
    sent_dest = jnp.sum(jnp.where(matches, slot_dest[None, :] + 1, 0), axis=1) - 1
    return (selector, sent_dest.reshape(shards, capacity))


def pack(selector, rows, shards, capacity):
    flattened = rows.reshape(rows.shape[0], rows.shape[1] * rows.shape[2])
    packed = jnp.dot(selector, flattened, preferred_element_type=jnp.float32).astype(jnp.bfloat16)
    return packed.reshape(shards, capacity, rows.shape[1], rows.shape[2])


def unpack(received, received_dest, own_index, per_shard):
    flat_dest = received_dest.reshape(-1)
    local = jnp.where(flat_dest >= 0, flat_dest - own_index * per_shard, -1)
    placer = (jnp.arange(per_shard)[:, None] == local[None, :]).astype(jnp.bfloat16)
    stacked = received.reshape(flat_dest.shape[0], received.shape[2] * received.shape[3])
    placed = jnp.dot(placer, stacked, preferred_element_type=jnp.float32).astype(jnp.bfloat16)
    return placed.reshape(per_shard, received.shape[2], received.shape[3])


def edge_windows(query_rows, keys, values, prev_keys, prev_values):
    tokens_here = query_rows.shape[0]
    width = query_rows.shape[1]
    blocks = keys.shape[0]
    padded = jnp.concatenate(
        [
            jnp.zeros((1, width), jnp.bfloat16),
            query_rows,
            jnp.zeros((SEGLEN - 1, width), jnp.bfloat16),
        ],
        axis=0,
    )
    padded = padded.reshape(blocks + 1, SEGLEN, width)
    all_keys = jnp.concatenate([prev_keys[None], keys], axis=0)
    all_values = jnp.concatenate([prev_values[None], values], axis=0)
    context = attend(padded, all_keys, all_values)
    return context.reshape((blocks + 1) * SEGLEN, width)[1 : tokens_here + 1]


def on_device(queries, key_weight, value_weight, enc_gain, neighbour_states, slot_dest):
    shards = lax.axis_size("seq")
    own_index = lax.axis_index("seq")
    query_rows = queries[0]
    tokens_here = query_rows.shape[0]
    blocks = tokens_here // SEGLEN
    per_shard = NEIGH * blocks
    capacity = per_shard // shards + 1
    selector, sent_dest = packing(slot_dest, shards, per_shard, capacity)
    received, received_dest = (
        lax.all_to_all(
            pack(selector, neighbour_states, shards, capacity),
            "seq",
            split_axis=0,
            concat_axis=0,
            tiled=True,
        ),
        lax.all_to_all(sent_dest, "seq", split_axis=0, concat_axis=0, tiled=True),
    )
    arranged = unpack(received, received_dest, own_index, per_shard)
    routed = lax.all_gather(arranged, ("phase", "mp"), axis=1, tiled=True)
    neighbours = normalize(routed, enc_gain)
    key_mat = key_weight[0]
    value_mat = value_weight[0]
    width = key_mat.shape[1]
    keys = project(neighbours, key_mat).reshape(blocks, NEIGH * NLEN, width)
    values = project(neighbours, value_mat).reshape(blocks, NEIGH * NLEN, width)
    prev_keys, prev_values = shifted((keys[blocks - 1], values[blocks - 1]), "seq", 1)
    joined = edge_windows(query_rows, keys, values, prev_keys, prev_values)
    position = jnp.arange(tokens_here) + 1
    window_index = own_index * blocks + position // SEGLEN
    silent = (position % SEGLEN != 0) & (window_index == 0)
    result = jnp.where(silent[:, None], jnp.zeros_like(joined), joined)
    return result[None]


def solution(mesh):
    in_specs = (
        P("phase", "seq", "mp"),
        P("phase", None, "mp"),
        P("phase", None, "mp"),
        P(),
        P("seq", ("phase", "mp"), None),
        P("seq"),
    )
    out_specs = P("phase", "seq", "mp")
    return jax.shard_map(
        on_device, mesh=mesh, in_specs=in_specs, out_specs=out_specs, check_vma=False
    )
```

profile of v0, /device:TPU:0, one launch (start us, length us, event | category | flops | bytes accessed | tf_op | source)
XLA Modules:
  0.0 137.3 jit_solution(5685725750526515950)
XLA Ops:
  6.5 0.7 broadcast_add_fusion.1
  8.2 0.7 sub.37
  8.8 6.3 %all-to-all-start = ((s32[4,1,5]{2,1,0:T(1,128)}), s32[4,1,5]{2,1,0:T(1,128)S(1)}, u32[]{:S(2)}, u32[]{:S(2)}) async-start(s32[4,1,5]{2,1,0:T(1,128)} %bitcast), calls=%async_computation | async-start | bytes 4096 | tf_op jit(solution)/shard_map/all_to_all | solution.py:110
  15.2 1.0 pad.7
  16.9 0.7 slice.17
  17.7 2.9 %all-to-all-done = s32[4,1,5]{2,1,0:T(1,128)S(1)} async-done(((s32[4,1,5]{2,1,0:T(1,128)}), s32[4,1,5]{2,1,0:T(1,128)S(1)}, u32[]{:S(2)}, u32[]{:S(2)}) %all-to-all-start) | async-done | bytes 112 | tf_op jit(solution)/shard_map/all_to_all | solution.py:110
  20.6 3.5 %all-to-all-start.1 = ((bf16[4,5,8,1024]{3,2,1,0:T(8,128)(2,1)}), bf16[4,5,8,1024]{3,2,1,0:T(8,128)(2,1)S(1)}, u32[]{:S(2)}, u32[]{:S(2)}) async-start(bf16[4,5,8,1024]{3,2,1,0:T(8,128)(2,1)} %bitcast.17), calls=%async_computation.1 | async-start | bytes 655360 | tf_op jit(solution)/shard_map/all_to_all | solution.py:103
  24.2 9.1 %all-to-all-done.1 = bf16[4,5,8,1024]{3,2,1,0:T(8,128)(2,1)S(1)} async-done(((bf16[4,5,8,1024]{3,2,1,0:T(8,128)(2,1)}), bf16[4,5,8,1024]{3,2,1,0:T(8,128)(2,1)S(1)}, u32[]{:S(2)}, u32[]{:S(2)}) %all-to-all-start.1) | async-done | bytes 327712 | tf_op jit(solution)/shard_map/all_to_all | solution.py:103
  33.8 0.9 copy.35
  34.7 27.0 %all-gather.2.cloned.1.call-done = bf16[16,64,1024]{2,1,0:T(8,128)(2,1)} async-done(((bf16[16,8,1024]{2,1,0:T(8,128)(2,1)}), bf16[16,64,1024]{2,1,0:T(8,128)(2,1)}) %all-gather.2.cloned.1.call-update) | async-done | bytes 2097168 | tf_op jit(solution)/shard_map/all_gather | solution.py:113
  61.7 2.2 %fusion.9 = f32[16,64]{1,0:T(8,128)S(1)} fusion(bf16[16,64,1024]{2,1,0:T(8,128)(2,1)} %all-gather.2.cloned.1.call-done), kind=kLoop, calls=%fused_computation.15 | loop fusion | flops 3144704 | bytes 2101248 | tf_op jit(solution)/shard_map/reduce_sum | solution.py:20
  64.0 2.1 %fusion.11 = bf16[16,64,1024]{2,1,0:T(8,128)(2,1)S(1)} fusion(bf16[16,64,1024]{2,1,0:T(8,128)(2,1)} %all-gather.2.cloned.1.call-done, f32[1024]{0:T(1024)S(1)} %copy-done.6, f32[16,64]{1,0:T(8,128)S(1)} %add_rsqrt_fusion), kind=kLoop, calls=%fused_computation.17 | loop fusion | flops 4194304 | bytes 4202496 | tf_op jit(solution)/shard_map/convert_element_type | solution.py:21
  66.1 4.7 %fusion.20 = bf16[1024,2048]{1,0:T(8,128)(2,1)S(1)} fusion(bf16[1024,1024]{1,0:T(8,128)(2,1)S(1)} %bitcast.64, bf16[1,1024,2048]{2,1,0:T(8,128)(2,1)S(1)} %copy-done.7), kind=kOutput, calls=%fused_computation.25 | convolution fusion | flops 4297064448 | bytes 10485760 | tf_op jit(solution)/shard_map/dot_general | solution.py:26
  70.9 0.9 slice.14
  71.8 3.7 %collective-permute-start.1 = (bf16[128,2048]{1,0:T(8,128)(2,1)}, bf16[128,2048]{1,0:T(8,128)(2,1)S(1)}, u32[]{:S(2)}, u32[]{:S(2)}) collective-permute-start(bf16[128,2048]{1,0:T(8,128)(2,1)} %slice.14), channel_id=1, source_target_pairs={{0,2},{2,4},{4,6},{1,3},{3,5},{5,7},{8,10},{10,12},{12,14},{9,11},... | collective-permute-start | bytes 1572872 | tf_op jit(solution)/shard_map/ppermute | solution.py:15
  75.4 4.7 %fusion.17 = bf16[1024,2048]{1,0:T(8,128)(2,1)S(1)} fusion(bf16[1024,1024]{1,0:T(8,128)(2,1)S(1)} %bitcast.65, bf16[1,1024,2048]{2,1,0:T(8,128)(2,1)S(1)} %copy-done.8), kind=kOutput, calls=%fused_computation.24 | convolution fusion | flops 4297064448 | bytes 10485760 | tf_op jit(solution)/shard_map/dot_general | solution.py:26
  80.2 0.9 slice.15
  81.1 1.3 copy-done.2
  82.4 3.6 %collective-permute-start = (bf16[128,2048]{1,0:T(8,128)(2,1)}, bf16[128,2048]{1,0:T(8,128)(2,1)S(1)}, u32[]{:S(2)}, u32[]{:S(2)}) collective-permute-start(bf16[128,2048]{1,0:T(8,128)(2,1)} %slice.15), channel_id=1, source_target_pairs={{0,2},{2,4},{4,6},{1,3},{3,5},{5,7},{8,10},{10,12},{12,14},{9,11},... | collective-permute-start | bytes 1572872 | tf_op jit(solution)/shard_map/ppermute | solution.py:15
  86.0 1.0 maximum_bitcast_fusion
  87.1 0.7 copy.31
  88.2 1.4 %copy.39 = bf16[128,8,16,128]{3,2,1,0:T(8,128)(2,1)S(1)} copy(bf16[128,8,16,128]{3,1,2,0:T(8,128)(2,1)S(1)} %bitcast.62) | data formatting | bytes 8388608
  89.7 3.2 %copy.26 = bf16[8,128,16,128]{3,1,2,0:T(8,128)(2,1)} copy(bf16[8,128,16,128]{3,2,1,0:T(8,128)(2,1)S(1)} %bitcast.56) | data formatting | bytes 8388608 | tf_op jit(solution)/shard_map/concatenate | solution.py:88
  92.8 1.4 %copy.37 = bf16[128,8,16,128]{3,2,1,0:T(8,128)(2,1)S(1)} copy(bf16[128,8,16,128]{3,1,2,0:T(8,128)(2,1)S(1)} %bitcast.61) | data formatting | bytes 8388608
  94.3 1.2 copy.28
  95.7 2.8 %collective-permute-done = bf16[128,2048]{1,0:T(8,128)(2,1)S(1)} collective-permute-done((bf16[128,2048]{1,0:T(8,128)(2,1)}, bf16[128,2048]{1,0:T(8,128)(2,1)S(1)}, u32[]{:S(2)}, u32[]{:S(2)}) %collective-permute-start) | collective-permute-done | bytes 524320 | tf_op jit(solution)/shard_map/ppermute | solution.py:15
  98.8 3.3 %fusion.1 = f32[9,16,64,128]{3,2,1,0:T(8,128)S(1)} fusion(bf16[8,128,16,128]{3,1,2,0:T(8,128)(2,1)S(1)} %copy.28, bf16[1,128,16,128]{3,1,2,0:T(8,128)(2,1)S(1)} %copy.27, bf16[9,64,16,128]{3,2,1,0:T(8,128)(2,1)S(1)} %bitcast.59), kind=kOutput, calls=%fused_computation.5 | convolution fusion | flops 304349184 | bytes 11796480 | tf_op jit(solution)/shard_map/wqhd,wkhd->whqk/dot_general | solution.py:35
  102.1 2.1 %copy-done.4 = f32[9,16,64,128]{3,2,1,0:T(8,128)} copy-done((f32[9,16,64,128]{3,2,1,0:T(8,128)}, f32[9,16,64,128]{3,2,1,0:T(8,128)S(1)}, u32[]{:S(2)}) %copy-start.4) | copy-done | bytes 4718616
  104.2 2.5 %fusion.51 = f32[9,16,64]{2,1,0:T(8,128)S(1)} fusion(f32[9,16,64,128]{3,2,1,0:T(8,128)S(1)} %fusion.1), kind=kOutput, calls=%fused_computation.71 | output fusion | flops 4718719 | bytes 4755456 | tf_op jit(solution)/shard_map/sub | solution.py:39
  106.7 19.5 %convert_bitcast_fusion = bf16[9,64,16,128]{3,1,2,0:T(8,128)(2,1)S(1)} fusion(bf16[8,128,16,128]{3,1,2,0:T(8,128)(2,1)} %copy.26, bf16[1,128,16,128]{3,1,2,0:T(8,128)(2,1)S(1)} %copy.25, f32[9,16,64]{2,1,0:T(8,128)S(1)} %fusion.51, f32[9,16,64,128]{3,2,1,0:T(8,128)} %copy-done.4), kind=kOutput, calls=%fused_computation.29 | convolution fusion | flops 318514304 | bytes 11833344 | tf_op jit(solution)/shard_map/whqk,wkhd->wqhd/dot_general | solution.py:41
  126.2 1.6 %copy.30 = bf16[9,64,16,128]{3,2,1,0:T(8,128)(2,1)S(1)} copy(bf16[9,64,16,128]{3,1,2,0:T(8,128)(2,1)S(1)} %convert_bitcast_fusion) | data formatting | bytes 4718592 | tf_op jit(solution)/shard_map/convert_element_type | solution.py:42
  128.5 2.0 %fusion.28 = bf16[1,512,2048]{2,1,0:T(8,128)(2,1)} fusion(bf16[576,2048]{1,0:T(8,128)(2,1)S(1)} %bitcast.60, pred[512]{0:T(512)(128)(4,1)S(1)} %fusion.44), kind=kLoop, calls=%fused_computation.33 | loop fusion | flops 1048576 | bytes 4194816 | tf_op jit(solution)/shard_map/broadcast_in_dim | solution.py:126
  (41 shorter events, 3.9 us)
Async XLA Ops:
  8.8 11.8 %all-to-all-start = ((s32[4,1,5]{2,1,0:T(1,128)}), s32[4,1,5]{2,1,0:T(1,128)S(1)}, u32[]{:S(2)}, u32[]{:S(2)}) async-start(s32[4,1,5]{2,1,0:T(1,128)} %bitcast), calls=%async_computation | async-start | bytes 4096 | tf_op jit(solution)/shard_map/all_to_all | solution.py:110
  16.2 47.8 %copy-start.6 = (f32[1024]{0:T(1024)S(1)}, f32[1024]{0:T(1024)}, u32[]{:S(2)}) copy-start(f32[1024]{0:T(1024)} %param.9) | copy-start | bytes 12292
  20.6 12.7 %all-to-all-start.1 = ((bf16[4,5,8,1024]{3,2,1,0:T(8,128)(2,1)}), bf16[4,5,8,1024]{3,2,1,0:T(8,128)(2,1)S(1)}, u32[]{:S(2)}, u32[]{:S(2)}) async-start(bf16[4,5,8,1024]{3,2,1,0:T(8,128)(2,1)} %bitcast.17), calls=%async_computation.1 | async-start | bytes 655360 | tf_op jit(solution)/shard_map/all_to_all | solution.py:103
  24.1 37.6 %all-gather.2.cloned.1.call-start = ((), (), s32[]{:S(2)}) async-start(), calls=%async_computation.2 | async-start | bytes 2359296 | tf_op jit(solution)/shard_map/all_gather | solution.py:113
  61.7 4.4 %copy-start.7 = (bf16[1,1024,2048]{2,1,0:T(8,128)(2,1)S(1)}, bf16[1,1024,2048]{2,1,0:T(8,128)(2,1)}, u32[]{:S(2)}) copy-start(bf16[1,1024,2048]{2,1,0:T(8,128)(2,1)} %param.7) | copy-start | bytes 12582916
  66.1 9.3 %copy-start.8 = (bf16[1,1024,2048]{2,1,0:T(8,128)(2,1)S(1)}, bf16[1,1024,2048]{2,1,0:T(8,128)(2,1)}, u32[]{:S(2)}) copy-start(bf16[1,1024,2048]{2,1,0:T(8,128)(2,1)} %param.8) | copy-start | bytes 12582916
  70.9 9.3 %copy-start = (bf16[1024,2048]{1,0:T(8,128)(2,1)}, bf16[1024,2048]{1,0:T(8,128)(2,1)S(1)}, u32[]{:S(2)}) copy-start(bf16[1024,2048]{1,0:T(8,128)(2,1)S(1)} %fusion.20) | copy-start | bytes 12582916
  71.8 14.3 %copy-start.5 = (bf16[1,512,2048]{2,1,0:T(8,128)(2,1)S(1)}, bf16[1,512,2048]{2,1,0:T(8,128)(2,1)}, u32[]{:S(2)}) copy-start(bf16[1,512,2048]{2,1,0:T(8,128)(2,1)} %param.6) | copy-start | bytes 6291460
  71.8 23.7 %collective-permute-start.1 = (bf16[128,2048]{1,0:T(8,128)(2,1)}, bf16[128,2048]{1,0:T(8,128)(2,1)S(1)}, u32[]{:S(2)}, u32[]{:S(2)}) collective-permute-start(bf16[128,2048]{1,0:T(8,128)(2,1)} %slice.14), channel_id=1, source_target_pairs={{0,2},{2,4},{4,6},{1,3},{3,5},{5,7},{8,10},{10,12},{12,14},{9,11},... | collective-permute-start | bytes 1572872 | tf_op jit(solution)/shard_map/ppermute | solution.py:15
  80.2 2.2 %copy-start.2 = (bf16[1024,2048]{1,0:T(8,128)(2,1)}, bf16[1024,2048]{1,0:T(8,128)(2,1)S(1)}, u32[]{:S(2)}) copy-start(bf16[1024,2048]{1,0:T(8,128)(2,1)S(1)} %fusion.17) | copy-start | bytes 12582916
  82.4 16.1 %collective-permute-start = (bf16[128,2048]{1,0:T(8,128)(2,1)}, bf16[128,2048]{1,0:T(8,128)(2,1)S(1)}, u32[]{:S(2)}, u32[]{:S(2)}) collective-permute-start(bf16[128,2048]{1,0:T(8,128)(2,1)} %slice.15), channel_id=1, source_target_pairs={{0,2},{2,4},{4,6},{1,3},{3,5},{5,7},{8,10},{10,12},{12,14},{9,11},... | collective-permute-start | bytes 1572872 | tf_op jit(solution)/shard_map/ppermute | solution.py:15
  86.0 2.2 %copy-start.3 = (bf16[1024,2048]{1,0:T(8,128)(2,1)S(1)}, bf16[1024,2048]{1,0:T(8,128)(2,1)}, u32[]{:S(2)}) copy-start(bf16[1024,2048]{1,0:T(8,128)(2,1)} %copy-done.2) | copy-start | bytes 12582916
  89.6 3.2 %copy-start.1 = (bf16[1024,2048]{1,0:T(8,128)(2,1)S(1)}, bf16[1024,2048]{1,0:T(8,128)(2,1)}, u32[]{:S(2)}) copy-start(bf16[1024,2048]{1,0:T(8,128)(2,1)} %copy-done) | copy-start | bytes 12582916
  102.1 2.1 %copy-start.4 = (f32[9,16,64,128]{3,2,1,0:T(8,128)}, f32[9,16,64,128]{3,2,1,0:T(8,128)S(1)}, u32[]{:S(2)}) copy-start(f32[9,16,64,128]{3,2,1,0:T(8,128)S(1)} %fusion.1) | copy-start | bytes 14155780
Sparse Core Ops, SparseCore 0:
  34.8 26.8 all-gather.1
where the time goes:
time: 138 us; the launch traced here: 137 us
  waiting for transfers between devices  41.9 us (30%)
  matrix products  32.7 us (24%)
  local copies, waits for them, and re-layouts  20.4 us (15%)
  starting transfers between devices  17.1 us (12%)
  between operations  13.7 us (10%)
  other arithmetic  11.6 us (8%)
    all_gather x1, waiting for transfers between devices, on_device(): routed = lax.all_gather(arranged, ('phase', 'mp'), axis=1, tiled=True)  27 us
    dot_general x1, matrix products, attend(): jnp.einsum('whqk,wkhd->wqhd', weights, value_four, preferred_element_type...  19.5 us
    unnamed x31, local copies, waits for them, and re-layouts  11.5 us
    dot_general x2, matrix products, project(): jnp.dot(flattened, weight, preferred_element_type=jnp.float32)  9.46 us
    all_to_all x1, waiting for transfers between devices, on_device(): lax.all_to_all(pack(selector, neighbour_states, shards, capacity), 'seq',...  9.08 us
    ppermute x2, starting transfers between devices, shifted(): return lax.ppermute(shard, axis, pairs)  7.23 us
    all_to_all x1, starting transfers between devices, on_device(): lax.all_to_all(sent_dest, 'seq', split_axis=0, concat_axis=0, tiled=True)  6.35 us
    all_to_all x1, starting transfers between devices, on_device(): lax.all_to_all(pack(selector, neighbour_states, shards, capacity), 'seq',...  3.45 us
  transfers between devices with their start and end apart: 5, of which 4 were waited for; matrix products, arithmetic and copies ran while one was open for 13% of the time, Pallas kernels for 0%

commit v1 on v0

--- a/solution.py
+++ b/solution.py
@@ -110,7 +110,15 @@
         lax.all_to_all(sent_dest, "seq", split_axis=0, concat_axis=0, tiled=True),
     )
     arranged = unpack(received, received_dest, own_index, per_shard)
-    routed = lax.all_gather(arranged, ("phase", "mp"), axis=1, tiled=True)
+    routed = jnp.concatenate(
+        jax.lax.all_to_all(
+            jnp.stack([arranged for _ in range(jax.lax.axis_size(("phase", "mp")))], 0),
+            ("phase", "mp"),
+            0,
+            0,
+        ),
+        1,
+    )
     neighbours = normalize(routed, enc_gain)
     key_mat = key_weight[0]
     value_mat = value_weight[0]

time: 138 us -> 122 us (0.88)
  blocking collectives: 0 us -> 29.2 us
  waiting for transfers between devices: 41.9 us -> 16.2 us
  between operations: 13.7 us -> 0.32 us
  other arithmetic: 11.6 us -> 8.25 us
  starting transfers between devices: 17.1 us -> 14.3 us
    all_to_all x0 -> x1, blocking collectives: none -> 29.2 us  [on_device(): jax.lax.all_to_all(jnp.stack([arranged for _ in range(jax.lax.axis_size((...]
    all_gather x1 -> x0, waiting for transfers between devices: 27 us -> none  [on_device(): routed = lax.all_gather(arranged, ('phase', 'mp'), axis=1, tiled=True)]
    ppermute x2, starting transfers between devices: 7.23 us -> 4.5 us  [shifted(): return lax.ppermute(shard, axis, pairs)]
    reduce_sum x1, other arithmetic: 2.22 us -> 0.48 us  [normalize(): meansq = jnp.mean(states * states, axis=-1, keepdims=True)]
    convert_element_type x1, other arithmetic: 2.13 us -> 0.54 us  [normalize(): return (states * lax.rsqrt(meansq + 1e-06) * gain).astype(jnp.bfloat16)]
  transfers between devices with their start and end apart: 5 -> 4, of which waited for: 4 -> 3; matrix products, arithmetic and copies ran while one was open for 13% -> 14% of each run, Pallas kernels for 0% -> 0%
where the time goes in v1:
time: 122 us
  matrix products  32.7 us (27%)
  blocking collectives  29.2 us (24%)
  local copies, waits for them, and re-layouts  21.1 us (17%)
  waiting for transfers between devices  16.2 us (13%)
  starting transfers between devices  14.3 us (12%)
  other arithmetic  8.25 us (7%)
    all_to_all x1, blocking collectives, on_device(): jax.lax.all_to_all(jnp.stack([arranged for _ in range(jax.lax.axis_size((...  29.2 us
    dot_general x1, matrix products, attend(): jnp.einsum('whqk,wkhd->wqhd', weights, value_four, preferred_element_type...  19.5 us
    unnamed x31, local copies, waits for them, and re-layouts  11.9 us
    dot_general x2, matrix products, project(): jnp.dot(flattened, weight, preferred_element_type=jnp.float32)  9.44 us
    all_to_all x1, waiting for transfers between devices, on_device(): lax.all_to_all(pack(selector, neighbour_states, shards, capacity), 'seq',...  9.13 us
    all_to_all x1, starting transfers between devices, on_device(): lax.all_to_all(sent_dest, 'seq', split_axis=0, concat_axis=0, tiled=True)  6.35 us
    ppermute x2, starting transfers between devices, shifted(): return lax.ppermute(shard, axis, pairs)  4.5 us
    ppermute x2, waiting for transfers between devices, shifted(): return lax.ppermute(shard, axis, pairs)  4.17 us
  transfers between devices with their start and end apart: 4, of which 3 were waited for; matrix products, arithmetic and copies ran while one was open for 14% of the time, Pallas kernels for 0%

profile of v1, /device:TPU:0, one launch (start us, length us, event | category | flops | bytes accessed | tf_op | source)
XLA Modules:
  0.0 122.0 jit_solution(542537540008947141)
XLA Ops:
  0.0 0.7 broadcast_add_fusion.1
  0.8 0.7 compare_select_fusion.4
  1.6 0.7 sub.37
  2.3 6.3 %all-to-all-start = ((s32[4,1,5]{2,1,0:T(1,128)}), s32[4,1,5]{2,1,0:T(1,128)S(1)}, u32[]{:S(2)}, u32[]{:S(2)}) async-start(s32[4,1,5]{2,1,0:T(1,128)} %bitcast), calls=%async_computation | async-start | bytes 4096 | tf_op jit(solution)/shard_map/all_to_all | solution.py:110
  8.7 1.0 pad.7
  10.4 0.7 slice.17
  11.1 2.9 %all-to-all-done = s32[4,1,5]{2,1,0:T(1,128)S(1)} async-done(((s32[4,1,5]{2,1,0:T(1,128)}), s32[4,1,5]{2,1,0:T(1,128)S(1)}, u32[]{:S(2)}, u32[]{:S(2)}) %all-to-all-start) | async-done | bytes 112 | tf_op jit(solution)/shard_map/all_to_all | solution.py:110
  14.1 3.5 %all-to-all-start.1 = ((bf16[4,5,8,1024]{3,2,1,0:T(8,128)(2,1)}), bf16[4,5,8,1024]{3,2,1,0:T(8,128)(2,1)S(1)}, u32[]{:S(2)}, u32[]{:S(2)}) async-start(bf16[4,5,8,1024]{3,2,1,0:T(8,128)(2,1)} %bitcast.18), calls=%async_computation.1 | async-start | bytes 655360 | tf_op jit(solution)/shard_map/all_to_all | solution.py:103
  17.7 9.1 %all-to-all-done.1 = bf16[4,5,8,1024]{3,2,1,0:T(8,128)(2,1)S(1)} async-done(((bf16[4,5,8,1024]{3,2,1,0:T(8,128)(2,1)}), bf16[4,5,8,1024]{3,2,1,0:T(8,128)(2,1)S(1)}, u32[]{:S(2)}, u32[]{:S(2)}) %all-to-all-start.1) | async-done | bytes 327712 | tf_op jit(solution)/shard_map/all_to_all | solution.py:103
  27.7 29.2 %all_to_all.16 = bf16[8,16,8,1024]{3,2,1,0:T(8,128)(2,1)S(1)} all-to-all(bf16[8,16,8,1024]{3,2,1,0:T(8,128)(2,1)S(1)} %stack.3), channel_id=1, replica_groups=mesh['phase'=4,'seq'=4,'mp'=2] {'phase','mp'}, dimensions={0} | all-to-all | bytes 4194304 | tf_op jit(solution)/shard_map/all_to_all | solution.py:114
  58.0 1.1 copy-done.7
  59.1 4.7 %fusion.20 = bf16[1024,2048]{1,0:T(8,128)(2,1)S(1)} fusion(bf16[1024,1024]{1,0:T(8,128)(2,1)S(1)} %bitcast.73, bf16[1,1024,2048]{2,1,0:T(8,128)(2,1)S(1)} %copy-done.7), kind=kOutput, calls=%fused_computation.25 | convolution fusion | flops 4297064448 | bytes 10485760 | tf_op jit(solution)/shard_map/dot_general | solution.py:26
  63.8 0.9 slice.14
  64.7 2.0 %collective-permute-start.1 = (bf16[128,2048]{1,0:T(8,128)(2,1)}, bf16[128,2048]{1,0:T(8,128)(2,1)S(1)}, u32[]{:S(2)}, u32[]{:S(2)}) collective-permute-start(bf16[128,2048]{1,0:T(8,128)(2,1)} %slice.14), channel_id=1, source_target_pairs={{0,2},{2,4},{4,6},{1,3},{3,5},{5,7},{8,10},{10,12},{12,14},{9,11},... | collective-permute-start | bytes 1572872 | tf_op jit(solution)/shard_map/ppermute | solution.py:15
  66.8 4.7 %fusion.17 = bf16[1024,2048]{1,0:T(8,128)(2,1)S(1)} fusion(bf16[1024,1024]{1,0:T(8,128)(2,1)S(1)} %bitcast.74, bf16[1,1024,2048]{2,1,0:T(8,128)(2,1)S(1)} %copy-done.8), kind=kOutput, calls=%fused_computation.24 | convolution fusion | flops 4297064448 | bytes 10485760 | tf_op jit(solution)/shard_map/dot_general | solution.py:26
  71.5 0.9 slice.15
  72.4 1.3 %copy-done.2 = bf16[1024,2048]{1,0:T(8,128)(2,1)} copy-done((bf16[1024,2048]{1,0:T(8,128)(2,1)}, bf16[1024,2048]{1,0:T(8,128)(2,1)S(1)}, u32[]{:S(2)}) %copy-start.2) | copy-done | bytes 4194328
  73.7 2.5 %collective-permute-start = (bf16[128,2048]{1,0:T(8,128)(2,1)}, bf16[128,2048]{1,0:T(8,128)(2,1)S(1)}, u32[]{:S(2)}, u32[]{:S(2)}) collective-permute-start(bf16[128,2048]{1,0:T(8,128)(2,1)} %slice.15), channel_id=1, source_target_pairs={{0,2},{2,4},{4,6},{1,3},{3,5},{5,7},{8,10},{10,12},{12,14},{9,11},... | collective-permute-start | bytes 1572872 | tf_op jit(solution)/shard_map/ppermute | solution.py:15
  76.2 1.0 maximum_bitcast_fusion
  77.3 0.7 copy.33
  78.4 1.4 %copy.41 = bf16[128,8,16,128]{3,2,1,0:T(8,128)(2,1)S(1)} copy(bf16[128,8,16,128]{3,1,2,0:T(8,128)(2,1)S(1)} %bitcast.71) | data formatting | bytes 8388608
  79.9 3.2 %copy.28 = bf16[8,128,16,128]{3,1,2,0:T(8,128)(2,1)} copy(bf16[8,128,16,128]{3,2,1,0:T(8,128)(2,1)S(1)} %bitcast.65) | data formatting | bytes 8388608 | tf_op jit(solution)/shard_map/concatenate | solution.py:88
  83.0 1.4 %copy.39 = bf16[128,8,16,128]{3,2,1,0:T(8,128)(2,1)S(1)} copy(bf16[128,8,16,128]{3,1,2,0:T(8,128)(2,1)S(1)} %bitcast.70) | data formatting | bytes 8388608
  84.5 1.2 copy.30
  85.9 4.2 %collective-permute-done = bf16[128,2048]{1,0:T(8,128)(2,1)S(1)} collective-permute-done((bf16[128,2048]{1,0:T(8,128)(2,1)}, bf16[128,2048]{1,0:T(8,128)(2,1)S(1)}, u32[]{:S(2)}, u32[]{:S(2)}) %collective-permute-start) | collective-permute-done | bytes 524320 | tf_op jit(solution)/shard_map/ppermute | solution.py:15
  90.4 3.3 %fusion.1 = f32[9,16,64,128]{3,2,1,0:T(8,128)S(1)} fusion(bf16[8,128,16,128]{3,1,2,0:T(8,128)(2,1)S(1)} %copy.30, bf16[1,128,16,128]{3,1,2,0:T(8,128)(2,1)S(1)} %copy.29, bf16[9,64,16,128]{3,2,1,0:T(8,128)(2,1)S(1)} %bitcast.68), kind=kOutput, calls=%fused_computation.3 | convolution fusion | flops 304349184 | bytes 11796480 | tf_op jit(solution)/shard_map/wqhd,wkhd->whqk/dot_general | solution.py:35
  93.7 2.1 %copy-done.4 = f32[9,16,64,128]{3,2,1,0:T(8,128)} copy-done((f32[9,16,64,128]{3,2,1,0:T(8,128)}, f32[9,16,64,128]{3,2,1,0:T(8,128)S(1)}, u32[]{:S(2)}) %copy-start.4) | copy-done | bytes 4718616
  95.8 2.5 %fusion.51 = f32[9,16,64]{2,1,0:T(8,128)S(1)} fusion(f32[9,16,64,128]{3,2,1,0:T(8,128)S(1)} %fusion.1), kind=kOutput, calls=%fused_computation.71 | output fusion | flops 4718719 | bytes 4755456 | tf_op jit(solution)/shard_map/sub | solution.py:39
  98.3 19.5 %convert_bitcast_fusion = bf16[9,64,16,128]{3,1,2,0:T(8,128)(2,1)S(1)} fusion(bf16[8,128,16,128]{3,1,2,0:T(8,128)(2,1)} %copy.28, bf16[1,128,16,128]{3,1,2,0:T(8,128)(2,1)S(1)} %copy.27, f32[9,16,64]{2,1,0:T(8,128)S(1)} %fusion.51, f32[9,16,64,128]{3,2,1,0:T(8,128)} %copy-done.4), kind=kOutput, calls=%fused_computation.29 | convolution fusion | flops 318514304 | bytes 11833344 | tf_op jit(solution)/shard_map/whqk,wkhd->wqhd/dot_general | solution.py:41
  117.8 1.6 %copy.32 = bf16[9,64,16,128]{3,2,1,0:T(8,128)(2,1)S(1)} copy(bf16[9,64,16,128]{3,1,2,0:T(8,128)(2,1)S(1)} %convert_bitcast_fusion) | data formatting | bytes 4718592 | tf_op jit(solution)/shard_map/convert_element_type | solution.py:42
  119.4 0.6 copy.48
  120.0 2.0 %fusion.28 = bf16[1,512,2048]{2,1,0:T(8,128)(2,1)} fusion(bf16[576,2048]{1,0:T(8,128)(2,1)S(1)} %bitcast.69, pred[512]{0:T(512)(128)(4,1)S(1)} %fusion.44), kind=kLoop, calls=%fused_computation.33 | loop fusion | flops 1048576 | bytes 4194816 | tf_op jit(solution)/shard_map/broadcast_in_dim | solution.py:134
  (40 shorter events, 4.0 us)
Async XLA Ops:
  2.3 11.8 %all-to-all-start = ((s32[4,1,5]{2,1,0:T(1,128)}), s32[4,1,5]{2,1,0:T(1,128)S(1)}, u32[]{:S(2)}, u32[]{:S(2)}) async-start(s32[4,1,5]{2,1,0:T(1,128)} %bitcast), calls=%async_computation | async-start | bytes 4096 | tf_op jit(solution)/shard_map/all_to_all | solution.py:110
  14.1 12.7 %all-to-all-start.1 = ((bf16[4,5,8,1024]{3,2,1,0:T(8,128)(2,1)}), bf16[4,5,8,1024]{3,2,1,0:T(8,128)(2,1)S(1)}, u32[]{:S(2)}, u32[]{:S(2)}) async-start(bf16[4,5,8,1024]{3,2,1,0:T(8,128)(2,1)} %bitcast.18), calls=%async_computation.1 | async-start | bytes 655360 | tf_op jit(solution)/shard_map/all_to_all | solution.py:103
  27.4 30.0 %copy-start.6 = (f32[1024]{0:T(1024)S(1)}, f32[1024]{0:T(1024)}, u32[]{:S(2)}) copy-start(f32[1024]{0:T(1024)} %param.9) | copy-start | bytes 12292
  56.9 2.2 %copy-start.7 = (bf16[1,1024,2048]{2,1,0:T(8,128)(2,1)S(1)}, bf16[1,1024,2048]{2,1,0:T(8,128)(2,1)}, u32[]{:S(2)}) copy-start(bf16[1,1024,2048]{2,1,0:T(8,128)(2,1)} %param.7) | copy-start | bytes 12582916
  59.1 7.7 %copy-start.8 = (bf16[1,1024,2048]{2,1,0:T(8,128)(2,1)S(1)}, bf16[1,1024,2048]{2,1,0:T(8,128)(2,1)}, u32[]{:S(2)}) copy-start(bf16[1,1024,2048]{2,1,0:T(8,128)(2,1)} %param.8) | copy-start | bytes 12582916
  63.8 7.7 %copy-start = (bf16[1024,2048]{1,0:T(8,128)(2,1)}, bf16[1024,2048]{1,0:T(8,128)(2,1)S(1)}, u32[]{:S(2)}) copy-start(bf16[1024,2048]{1,0:T(8,128)(2,1)S(1)} %fusion.20) | copy-start | bytes 12582916
  64.7 11.6 %copy-start.5 = (bf16[1,512,2048]{2,1,0:T(8,128)(2,1)S(1)}, bf16[1,512,2048]{2,1,0:T(8,128)(2,1)}, u32[]{:S(2)}) copy-start(bf16[1,512,2048]{2,1,0:T(8,128)(2,1)} %param.6) | copy-start | bytes 6291460
  64.7 21.0 %collective-permute-start.1 = (bf16[128,2048]{1,0:T(8,128)(2,1)}, bf16[128,2048]{1,0:T(8,128)(2,1)S(1)}, u32[]{:S(2)}, u32[]{:S(2)}) collective-permute-start(bf16[128,2048]{1,0:T(8,128)(2,1)} %slice.14), channel_id=1, source_target_pairs={{0,2},{2,4},{4,6},{1,3},{3,5},{5,7},{8,10},{10,12},{12,14},{9,11},... | collective-permute-start | bytes 1572872 | tf_op jit(solution)/shard_map/ppermute | solution.py:15
  71.5 2.2 %copy-start.2 = (bf16[1024,2048]{1,0:T(8,128)(2,1)}, bf16[1024,2048]{1,0:T(8,128)(2,1)S(1)}, u32[]{:S(2)}) copy-start(bf16[1024,2048]{1,0:T(8,128)(2,1)S(1)} %fusion.17) | copy-start | bytes 12582916
  73.7 16.4 %collective-permute-start = (bf16[128,2048]{1,0:T(8,128)(2,1)}, bf16[128,2048]{1,0:T(8,128)(2,1)S(1)}, u32[]{:S(2)}, u32[]{:S(2)}) collective-permute-start(bf16[128,2048]{1,0:T(8,128)(2,1)} %slice.15), channel_id=1, source_target_pairs={{0,2},{2,4},{4,6},{1,3},{3,5},{5,7},{8,10},{10,12},{12,14},{9,11},... | collective-permute-start | bytes 1572872 | tf_op jit(solution)/shard_map/ppermute | solution.py:15
  76.2 2.2 %copy-start.3 = (bf16[1024,2048]{1,0:T(8,128)(2,1)S(1)}, bf16[1024,2048]{1,0:T(8,128)(2,1)}, u32[]{:S(2)}) copy-start(bf16[1024,2048]{1,0:T(8,128)(2,1)} %copy-done.2) | copy-start | bytes 12582916
  79.8 3.2 %copy-start.1 = (bf16[1024,2048]{1,0:T(8,128)(2,1)S(1)}, bf16[1024,2048]{1,0:T(8,128)(2,1)}, u32[]{:S(2)}) copy-start(bf16[1024,2048]{1,0:T(8,128)(2,1)} %copy-done) | copy-start | bytes 12582916
  93.7 2.1 %copy-start.4 = (f32[9,16,64,128]{3,2,1,0:T(8,128)}, f32[9,16,64,128]{3,2,1,0:T(8,128)S(1)}, u32[]{:S(2)}) copy-start(f32[9,16,64,128]{3,2,1,0:T(8,128)S(1)} %fusion.1) | copy-start | bytes 14155780
